TPU v7x, 256 devices: a whole 4x4x8 slice. The times are simulated.
256 devices in a mesh: subj: 8 (over x, core), space: 32 (over y, z).
Axes of the slice: x: 4, y: 4, z: 8, core: 2. Of those that a mesh axis runs over, the one named last changes fastest.
Arguments:
- images: bfloat16 [16, 2048, 16, 128], P('subj', 'space'), may hold values from -6 to 6
- velocity: float32 [3, 16, 2048, 16, 128], P(None, 'subj', 'space'), may hold values from -4 to 4
- weights: bfloat16 [3, 16, 2048, 16, 128], P(None, 'subj', 'space'), may hold values from 0 to 1
- template: float32 [2048, 16, 128], P('space', 'subj'), may hold values from -6 to 6
- owners: int32 [16, 2048, 1], P('subj', 'space'), may hold values from 0 to 31; in each aligned block of 64 rows (0 to 63, 64 to 127, ..., all dimensions but the last counted through in order) at most 4 rows name the same one
- local_rows: int32 [16, 2048], P('subj', 'space'), may hold values from 0 to 63
- tile_counts: int32 [16, 32], P('subj', 'space'), may hold values from 32 to 64
Outputs:
- new_velocity: float32 [3, 16, 2048, 16, 128], P(None, 'subj', 'space')
- new_template: float32 [2048, 16, 128], P('space', 'subj')
Inputs may be any that keep to these rules, and one draw needn't show every extreme that they name: `owners`: for each subject and each aligned block of 64 tiles, no value appears more than 4 times, and some value appears exactly 4 times.
All inputs are finite; a program needn't handle non-finite values.
Results may differ from a plain program's by a relative error of at most 0.0006.
Values may be sent and summed in bfloat16 or wider, within the bound.
A program may use at most 64 MiB of HBM per device.

v0:
```python
import jax
import jax.numpy as jnp
from jax import lax
from jax.sharding import PartitionSpec as P

BX = 4
BY = 4
ITERS = 2
ridge = 0.25


def extended(block, sides, width):
    for axis, dim in sides:
        count = lax.axis_size(axis)
        forward = [(i, i + 1) for i in range(count - 1)]
        backward = [(target, source) for source, target in forward]
        low = lax.ppermute(
            lax.slice_in_dim(block, block.shape[dim] - width, None, axis=dim), axis, forward
        )
        high = lax.ppermute(lax.slice_in_dim(block, 0, width, axis=dim), axis, backward)
        block = jnp.concatenate([low, block, high], axis=dim)
    return block


def shift_up(field, axis):
    body_part = lax.slice_in_dim(field, 1, field.shape[axis], axis=axis)
    edge = jnp.zeros_like(lax.slice_in_dim(field, 0, 1, axis=axis))
    return jnp.concatenate([body_part, edge], axis)


def shift_down(field, axis):
    body_part = lax.slice_in_dim(field, 0, field.shape[axis] - 1, axis=axis)
    edge = jnp.zeros_like(lax.slice_in_dim(field, 0, 1, axis=axis))
    return jnp.concatenate([edge, body_part], axis)


def trilinear(brick, frac_x, frac_y, frac_z):
    depth = brick.ndim
    total = jnp.zeros_like(brick)
    for offset_x in (0, 1):
        moved_x = brick if offset_x == 0 else shift_up(brick, depth - 3)
        weight_x = 1.0 - frac_x if offset_x == 0 else frac_x
        for offset_y in (0, 1):
            moved = moved_x if offset_y == 0 else shift_up(moved_x, depth - 2)
            weight_y = 1.0 - frac_y if offset_y == 0 else frac_y
            along_z = (1.0 - frac_z) * moved + frac_z * shift_up(moved, depth - 1)
            total = total + weight_x * weight_y * along_z
    return total


def gradients(field):
    depth = field.ndim
    return jnp.stack(
        [
            0.5 * (shift_up(field, depth - 3 + offset) - shift_down(field, depth - 3 + offset))
            for offset in range(3)
        ]
    )


def smooth_z(field):
    depth = field.ndim
    return 0.25 * shift_down(field, depth - 1) + 0.5 * field + 0.25 * shift_up(field, depth - 1)


def predict(warped, grads, field):
    return warped + (grads[0] * field[0] + grads[1] * field[1]) + grads[2] * field[2]


def body(images, velocity, weights, template, owners, local_rows, tile_counts):
    spaces = lax.axis_size("space")
    groups = lax.axis_size("subj")
    subj_dev = images.shape[0]
    rows_dev = images.shape[1]
    plane = images.shape[2]
    depth_z = images.shape[3]
    cap = 2 * rows_dev // spaces
    subjects = subj_dev * groups
    position = jnp.arange(rows_dev, dtype=jnp.int32)[None, :]
    first = tile_counts // 2
    alive = (position < first) | (position >= rows_dev - (tile_counts - first))
    owner = owners[:, :, 0]
    hits = (owner[:, :, None] == jnp.arange(spaces, dtype=jnp.int32)[None, None, :]).astype(
        jnp.int32
    )
    hits = hits * alive.astype(jnp.int32)[:, :, None]
    before = jnp.cumsum(hits, axis=1) - hits
    place = jnp.sum(before * hits, axis=2)
    slot = jnp.where(alive, owner * cap + place, spaces * cap)
    request = jnp.zeros((subj_dev, spaces * cap), jnp.int32)
    request = request.at[jnp.arange(subj_dev)[:, None], slot].set(local_rows, mode="drop")
    request = request.reshape(subj_dev, spaces, cap)
    wanted = lax.all_to_all(request, "space", split_axis=1, concat_axis=1, tiled=True)
    returned = lax.all_to_all(
        jax.vmap(lambda image, index: image[index])(images, wanted),
        "space",
        split_axis=1,
        concat_axis=1,
        tiled=True,
    )
    returned = returned.reshape(subj_dev, spaces * cap, plane, depth_z)
    read_slot = jnp.minimum(slot, spaces * cap - 1)
    fetched = jax.vmap(lambda table, index: table[index])(returned, read_slot)
    live = alive.astype(jnp.float32)
    brick = fetched.astype(jnp.float32).reshape(subj_dev, rows_dev, BX, BY, depth_z)
    frac = weights.astype(jnp.float32).reshape(3, subj_dev, rows_dev, BX, BY, depth_z)
    warped = trilinear(brick, frac[0], frac[1], frac[2]) * live[:, :, None, None, None]
    grads = gradients(warped)
    whole = lax.all_gather(template, "subj", axis=1, tiled=True)
    current = whole.reshape(rows_dev, BX, BY, depth_z)
    field = velocity.reshape(3, subj_dev, rows_dev, BX, BY, depth_z)
    piece = plane // groups
    result = template
    for step in range(ITERS):
        predicted = predict(warped, grads, field)
        ratio = (predicted - current[None]) / (
            grads[0] * grads[0] + grads[1] * grads[1] + grads[2] * grads[2] + ridge
        )
        update = grads * ratio[None]
        padded = extended(update, (("space", 2),), 1)
        rowwise = 0.25 * padded[:, :, :-2] + 0.5 * update + 0.25 * padded[:, :, 2:]
        field = field - smooth_z(rowwise)
        local_sum = jnp.sum(predict(warped, grads, field), axis=0).reshape(rows_dev, plane, depth_z)
        total = lax.psum(local_sum, "subj") / subjects
        current = total.reshape(rows_dev, BX, BY, depth_z)
        result = lax.dynamic_slice_in_dim(total, lax.axis_index("subj") * piece, piece, 1)
    return (field.reshape(3, subj_dev, rows_dev, plane, depth_z), result)


def solution(mesh):
    in_specs = (
        P("subj", "space", None, None),
        P(None, "subj", "space", None, None),
        P(None, "subj", "space", None, None),
        P("space", "subj", None),
        P("subj", "space", None),
        P("subj", "space"),
        P("subj", "space"),
    )
    out_specs = (P(None, "subj", "space", None, None), P("space", "subj", None))
    return jax.shard_map(body, mesh=mesh, in_specs=in_specs, out_specs=out_specs, check_vma=False)
```

profile of v0, /device:TPU:8, one launch (start us, length us, event | category | flops | bytes accessed | tf_op | source)
XLA Modules:
  0.0 271.9 jit_solution(7685412767636631632)
XLA Ops:
  7.2 0.7 subtract_bitcast_fusion
  7.9 0.1 fusion.42
  8.0 0.8 fusion.32
  8.8 0.1 reduce_window_sum.11
  8.9 0.9 fusion.31
  9.7 0.8 fusion.38
  10.5 0.1 reshape.240
  10.6 0.8 reshape.242
  11.4 6.4 %scatter_fusion = s32[2,128]{1,0:T(2,128)S(1)} fusion(s32[2,128]{1,0:T(2,128)S(1)} %broadcast_in_dim.10, s32[128]{0:T(128)S(1)} %reshape.240, s32[128]{0:T(128)S(1)} %reshape.242), kind=kCustom, calls=%fused_computation.2 | custom fusion | bytes 2560 | tf_op jit(solution)/shard_map/scatter | solution.py:91
  17.8 0.1 reshape.222
  17.9 20.2 %all_to_all.10 = s32[2,32,4]{2,0,1:T(2,128)S(1)} all-to-all(s32[2,32,4]{2,0,1:T(2,128)S(1)} %copy.24), channel_id=1, replica_groups=mesh['subj'=8,'space'=32] {'space'}, dimensions={1} | all-to-all | bytes 2048 | tf_op jit(solution)/shard_map/all_to_all | solution.py:93
  38.1 0.1 copy.25
  38.2 0.1 copy.28
  38.3 0.1 reshape.228
  38.4 1.2 gather_fusion
  39.7 1.1 copy.29
  40.8 5.8 %all-to-all-start.1 = ((bf16[2,32,4,16,128]{4,3,2,0,1:T(8,128)(2,1)}), bf16[2,32,4,16,128]{4,3,2,0,1:T(8,128)(2,1)}, u32[]{:S(2)}, u32[]{:S(2)}) async-start(bf16[2,32,4,16,128]{4,3,2,0,1:T(8,128)(2,1)} %copy.29), calls=%async_computation.1 | async-start | bytes 2097152 | tf_op jit(solution)/shard_map/all_to_all | solution.py:94
  46.7 0.1 reshape.234
  46.8 13.5 %all_gather.3 = f32[64,16,128]{2,0,1:T(8,128)S(1)} all-gather(f32[64,2,128]{2,0,1:T(8,128)S(1)} %copy.31), channel_id=1, replica_groups=mesh['subj'=8,'space'=32] {'subj'}, dimensions={1}, use_global_device_ids=true | all-gather | bytes 589824 | tf_op jit(solution)/shard_map/all_gather | solution.py:109
  60.2 1.2 copy.32
  61.4 1.6 fusion.52
  63.0 1.1 copy-done.8
  64.0 1.7 fusion.51
  65.8 5.9 %all-to-all-done.1 = bf16[2,32,4,16,128]{4,3,2,0,1:T(8,128)(2,1)} async-done(((bf16[2,32,4,16,128]{4,3,2,0,1:T(8,128)(2,1)}), bf16[2,32,4,16,128]{4,3,2,0,1:T(8,128)(2,1)}, u32[]{:S(2)}, u32[]{:S(2)}) %all-to-all-start.1) | async-done | bytes 1048608 | tf_op jit(solution)/shard_map/all_to_all | solution.py:94
  71.7 1.4 copy.30
  73.1 0.9 gather_fusion.1
  74.0 0.1 slice.172
  74.2 0.3 slice.171
  74.4 0.3 slice.170
  74.8 0.2 pad_slice_fusion
  75.0 1.0 pad_slice_fusion.1
  76.0 0.6 pad_slice_fusion.3
  76.7 2.3 fusion.12
  79.0 0.6 fusion.53
  79.7 0.4 fusion.54
  80.1 0.3 fusion.55
  80.4 0.5 copy-done.14
  80.9 0.3 copy-done.15
  81.2 0.6 copy-done.16
  81.8 0.1 copy-done.19
  81.9 1.9 subtract_divide_fusion.1
  83.9 0.9 broadcast_multiply_fusion.1
  84.8 0.1 copy-done.11
  84.9 5.0 %collective-permute-start = (f32[3,2,1,4,4,128]{5,4,3,2,1,0:T(4,128)S(1)}, f32[3,2,1,4,4,128]{5,4,3,2,1,0:T(4,128)S(1)}, u32[]{:S(2)}, u32[]{:S(2)}) collective-permute-start(f32[3,2,1,4,4,128]{5,4,3,2,1,0:T(4,128)S(1)} %get-tuple-element.17), channel_id=1, source_target_pairs={{0,1},{1,2},{2,3},{3,4},{4,5},{5,6},{6,7},{7,8},{8,9},{9,10},{10,1... | collective-permute-start | bytes 147464 | tf_op jit(solution)/shard_map/ppermute | solution.py:17
  89.9 3.1 %collective-permute-start.1 = (f32[3,2,1,4,4,128]{5,4,3,2,1,0:T(4,128)S(1)}, f32[3,2,1,4,4,128]{5,4,3,2,1,0:T(4,128)S(1)}, u32[]{:S(2)}, u32[]{:S(2)}) collective-permute-start(f32[3,2,1,4,4,128]{5,4,3,2,1,0:T(4,128)S(1)} %get-tuple-element.18), channel_id=1, source_target_pairs={{1,0},{2,1},{3,2},{4,3},{5,4},{6,5},{7,6},{8,7},{9,8},{10,9},{11,1... | collective-permute-start | bytes 147464 | tf_op jit(solution)/shard_map/ppermute | solution.py:20
  93.1 2.9 %collective-permute-done.1 = f32[3,2,1,4,4,128]{5,4,3,2,1,0:T(4,128)S(1)} collective-permute-done((f32[3,2,1,4,4,128]{5,4,3,2,1,0:T(4,128)S(1)}, f32[3,2,1,4,4,128]{5,4,3,2,1,0:T(4,128)S(1)}, u32[]{:S(2)}, u32[]{:S(2)}) %collective-permute-start.1) | collective-permute-done | bytes 49184 | tf_op jit(solution)/shard_map/ppermute | solution.py:20
  95.9 2.2 fusion.5
  98.2 2.1 fusion.49
  100.3 4.2 %add_subtract_fusion.1 = f32[3,2,64,4,4,128]{5,4,3,2,1,0:T(4,128)S(1)} fusion(f32[3,2,64,4,4,128]{5,4,3,2,1,0:T(4,128)S(1)} %bitcast.99, f32[3,2,64,4,4,127]{5,4,3,2,1,0:T(4,128)S(1)} %get-tuple-element.16, f32[3,2,64,4,4,127]{5,4,3,2,1,0:T(4,128)S(1)} %get-tuple-element.15, f32[3,2,1,4,4,128]{5,4,3,2,1,0:T(4,128)S(1)} %collective-permute-done.1, ...), kind=kLoop, calls=%fused_computation.17 | loop fusion | flops 10223616 | bytes 15777792 | tf_op jit(solution)/shard_map/sub | solution.py:122
  104.5 3.3 %fusion.45 = (f32[64,4,4,128]{3,2,1,0:T(4,128)}, f32[2,64,4,4,128]{4,3,2,1,0:T(4,128)}) fusion(f32[2,64,4,4,128]{4,3,2,1,0:T(4,128)S(1)} %get-tuple-element.6, f32[3,2,64,4,4,128]{5,4,3,2,1,0:T(4,128)S(1)} %add_subtract_fusion.1, f32[2,64,4,4,128]{4,3,2,1,0:T(4,128)S(1)} %fusion.12, f32[2,64,4,4,128]{4,3,2,1,0:T(4,128)S(1)} %get-tuple-element.5, ...), kind=kLoop, calls=%fused_computation.94 | loop fusion | flops 2228224 | bytes 9437184 | tf_op jit(solution)/shard_map/reduce_sum | solution.py:123
  107.9 0.0 all-reduce.22.cloned.1.call-start
  107.9 65.1 %all-reduce.20.cloned.1.call-done = f32[64,16,128]{2,1,0:T(8,128)} async-done(((f32[64,16,128]{2,1,0:T(8,128)}), f32[64,16,128]{2,1,0:T(8,128)}) %all-reduce.20.cloned.1.call-update) | async-done | bytes 524304 | tf_op jit(solution)/shard_map/psum | solution.py:124
  173.0 1.1 broadcast_multiply_fusion.2
  174.1 2.6 subtract_divide_fusion
  176.8 0.9 broadcast_multiply_fusion
  177.7 3.5 %collective-permute-start.2 = (f32[3,2,1,4,4,128]{5,4,3,2,1,0:T(4,128)S(1)}, f32[3,2,1,4,4,128]{5,4,3,2,1,0:T(4,128)S(1)}, u32[]{:S(2)}, u32[]{:S(2)}) collective-permute-start(f32[3,2,1,4,4,128]{5,4,3,2,1,0:T(4,128)S(1)} %get-tuple-element.13), channel_id=1, source_target_pairs={{0,1},{1,2},{2,3},{3,4},{4,5},{5,6},{6,7},{7,8},{8,9},{9,10},{10,1... | collective-permute-start | bytes 147464 | tf_op jit(solution)/shard_map/ppermute | solution.py:17
  181.1 4.7 %collective-permute-start.3 = (f32[3,2,1,4,4,128]{5,4,3,2,1,0:T(4,128)S(1)}, f32[3,2,1,4,4,128]{5,4,3,2,1,0:T(4,128)S(1)}, u32[]{:S(2)}, u32[]{:S(2)}) collective-permute-start(f32[3,2,1,4,4,128]{5,4,3,2,1,0:T(4,128)S(1)} %get-tuple-element.14), channel_id=1, source_target_pairs={{1,0},{2,1},{3,2},{4,3},{5,4},{6,5},{7,6},{8,7},{9,8},{10,9},{11,1... | collective-permute-start | bytes 147464 | tf_op jit(solution)/shard_map/ppermute | solution.py:20
  185.9 1.5 collective-permute-done.3
  187.4 2.2 fusion.1
  189.6 2.1 fusion.47
  191.8 4.2 %add_subtract_fusion = f32[3,2,64,4,4,128]{5,4,3,2,1,0:T(4,128)S(1)} fusion(f32[3,2,64,4,4,128]{5,4,3,2,1,0:T(4,128)S(1)} %copy-done.5, f32[3,2,64,4,4,127]{5,4,3,2,1,0:T(4,128)S(1)} %get-tuple-element.12, f32[3,2,64,4,4,127]{5,4,3,2,1,0:T(4,128)S(1)} %get-tuple-element.11, f32[3,2,1,4,4,128]{5,4,3,2,1,0:T(4,128)S(1)} %collective-permute-done.3, ...), kind=kLoop, calls=%fused_computation.16 | loop fusion | flops 10223616 | bytes 15777792 | tf_op jit(solution)/shard_map/sub | solution.py:122
  196.0 2.3 fusion.15
  198.4 65.1 %all-reduce.22.cloned.1.call-done = f32[64,16,128]{2,1,0:T(8,128)} async-done(((f32[64,16,128]{2,1,0:T(8,128)}), f32[64,16,128]{2,1,0:T(8,128)}) %all-reduce.22.cloned.1.call-update) | async-done | bytes 524304 | tf_op jit(solution)/shard_map/psum | solution.py:124
  263.4 1.6 dynamic-slice_multiply_fusion
  (48 shorter events, 0.2 us)
Async XLA Ops:
  7.2 31.3 %copy-start = (bf16[2,64,16,128]{3,2,1,0:T(8,128)(2,1)S(1)}, bf16[2,64,16,128]{3,2,1,0:T(8,128)(2,1)}, u32[]{:S(2)}) copy-start(bf16[2,64,16,128]{3,2,1,0:T(8,128)(2,1)} %param.7) | copy-start | bytes 1572868
  38.4 8.3 %copy-start.20 = (f32[64,2,128]{2,1,0:T(2,128)S(1)}, f32[64,2,128]{2,1,0:T(2,128)}, u32[]{:S(2)}) copy-start(f32[64,2,128]{2,1,0:T(2,128)} %param.10) | copy-start | bytes 196612
  39.7 21.7 %copy-start.13 = (bf16[3,2,64,16,128]{4,3,2,1,0:T(8,128)(2,1)S(1)}, bf16[3,2,64,16,128]{4,3,2,1,0:T(8,128)(2,1)}, u32[]{:S(2)}) copy-start(bf16[3,2,64,16,128]{4,3,2,1,0:T(8,128)(2,1)} %param.9) | copy-start | bytes 4718596
  40.8 30.8 %all-to-all-start.1 = ((bf16[2,32,4,16,128]{4,3,2,0,1:T(8,128)(2,1)}), bf16[2,32,4,16,128]{4,3,2,0,1:T(8,128)(2,1)}, u32[]{:S(2)}, u32[]{:S(2)}) async-start(bf16[2,32,4,16,128]{4,3,2,0,1:T(8,128)(2,1)} %copy.29), calls=%async_computation.1 | async-start | bytes 2097152 | tf_op jit(solution)/shard_map/all_to_all | solution.py:94
  46.6 126.4 %all-reduce.20.cloned.1.call-start = ((), (), s32[]{:S(2)}) async-start(), calls=%async_computation.2 | async-start | bytes 1048576 | tf_op jit(solution)/shard_map/psum | solution.py:124
  61.4 2.6 copy-start.8
  75.0 1.6 copy-start.17
  75.0 1.6 copy-start.18
  79.6 1.2 copy-start.14
  79.7 1.5 copy-start.15
  79.7 2.1 copy-start.16
  79.7 2.2 copy-start.19
  80.4 24.1 %copy-start.6 = (f32[2,64,3,4,128]{4,3,2,1,0:T(4,128)}, f32[2,64,3,4,128]{4,3,2,1,0:T(4,128)S(1)}, u32[]{:S(2)}) copy-start(f32[2,64,3,4,128]{4,3,2,1,0:T(4,128)S(1)} %get-tuple-element.31) | copy-start | bytes 2359300
  83.9 1.0 copy-start.11
  83.9 20.6 %copy-start.2 = (f32[2,64,4,4,128]{4,3,2,1,0:T(4,128)}, f32[2,64,4,4,128]{4,3,2,1,0:T(4,128)S(1)}, u32[]{:S(2)}) copy-start(f32[2,64,4,4,128]{4,3,2,1,0:T(4,128)S(1)} %get-tuple-element.6) | copy-start | bytes 3145732
  84.9 8.1 %collective-permute-start = (f32[3,2,1,4,4,128]{5,4,3,2,1,0:T(4,128)S(1)}, f32[3,2,1,4,4,128]{5,4,3,2,1,0:T(4,128)S(1)}, u32[]{:S(2)}, u32[]{:S(2)}) collective-permute-start(f32[3,2,1,4,4,128]{5,4,3,2,1,0:T(4,128)S(1)} %get-tuple-element.17), channel_id=1, source_target_pairs={{0,1},{1,2},{2,3},{3,4},{4,5},{5,6},{6,7},{7,8},{8,9},{9,10},{10,1... | collective-permute-start | bytes 147464 | tf_op jit(solution)/shard_map/ppermute | solution.py:17
  89.9 6.0 %collective-permute-start.1 = (f32[3,2,1,4,4,128]{5,4,3,2,1,0:T(4,128)S(1)}, f32[3,2,1,4,4,128]{5,4,3,2,1,0:T(4,128)S(1)}, u32[]{:S(2)}, u32[]{:S(2)}) collective-permute-start(f32[3,2,1,4,4,128]{5,4,3,2,1,0:T(4,128)S(1)} %get-tuple-element.18), channel_id=1, source_target_pairs={{1,0},{2,1},{3,2},{4,3},{5,4},{6,5},{7,6},{8,7},{9,8},{10,9},{11,1... | collective-permute-start | bytes 147464 | tf_op jit(solution)/shard_map/ppermute | solution.py:20
  98.2 2.2 copy-start.9
  104.5 3.3 %copy-start.4 = (f32[3,2,64,4,4,128]{5,4,3,2,1,0:T(4,128)}, f32[3,2,64,4,4,128]{5,4,3,2,1,0:T(4,128)S(1)}, u32[]{:S(2)}) copy-start(f32[3,2,64,4,4,128]{5,4,3,2,1,0:T(4,128)S(1)} %add_subtract_fusion.1) | copy-start | bytes 9437188
  107.9 155.5 %all-reduce.22.cloned.1.call-start = ((), (), s32[]{:S(2)}) async-start(), calls=%async_computation.3 | async-start | bytes 1048576 | tf_op jit(solution)/shard_map/psum | solution.py:124
  174.1 2.7 copy-start.3
  174.1 2.7 copy-start.12
  177.7 8.2 %collective-permute-start.2 = (f32[3,2,1,4,4,128]{5,4,3,2,1,0:T(4,128)S(1)}, f32[3,2,1,4,4,128]{5,4,3,2,1,0:T(4,128)S(1)}, u32[]{:S(2)}, u32[]{:S(2)}) collective-permute-start(f32[3,2,1,4,4,128]{5,4,3,2,1,0:T(4,128)S(1)} %get-tuple-element.13), channel_id=1, source_target_pairs={{0,1},{1,2},{2,3},{3,4},{4,5},{5,6},{6,7},{7,8},{8,9},{9,10},{10,1... | collective-permute-start | bytes 147464 | tf_op jit(solution)/shard_map/ppermute | solution.py:17
  181.1 6.2 %collective-permute-start.3 = (f32[3,2,1,4,4,128]{5,4,3,2,1,0:T(4,128)S(1)}, f32[3,2,1,4,4,128]{5,4,3,2,1,0:T(4,128)S(1)}, u32[]{:S(2)}, u32[]{:S(2)}) collective-permute-start(f32[3,2,1,4,4,128]{5,4,3,2,1,0:T(4,128)S(1)} %get-tuple-element.14), channel_id=1, source_target_pairs={{1,0},{2,1},{3,2},{4,3},{5,4},{6,5},{7,6},{8,7},{9,8},{10,9},{11,1... | collective-permute-start | bytes 147464 | tf_op jit(solution)/shard_map/ppermute | solution.py:20
  189.6 2.2 copy-start.5
  191.8 4.2 %copy-start.7 = (f32[2,64,3,4,128]{4,3,2,1,0:T(4,128)S(1)}, f32[2,64,3,4,128]{4,3,2,1,0:T(4,128)}, u32[]{:S(2)}) copy-start(f32[2,64,3,4,128]{4,3,2,1,0:T(4,128)} %copy-done.6) | copy-start | bytes 2359300
  191.8 73.2 %copy-start.1 = (bf16[2,64,16,128]{3,2,1,0:T(8,128)(2,1)S(1)}, bf16[2,64,16,128]{3,2,1,0:T(8,128)(2,1)}, u32[]{:S(2)}) copy-start(bf16[2,64,16,128]{3,2,1,0:T(8,128)(2,1)} %param.7) | copy-start | bytes 1572868
  196.0 2.3 copy-start.10
Sparse Core Ops, SparseCore 0:
  108.0 64.9 all-reduce.19
  198.5 64.9 all-reduce.21
where the time goes:
time: 272 us
  waiting for transfers between devices  140 us (51%)
  blocking collectives  33.6 us (12%)
  other arithmetic  33.1 us (12%)
  local copies, waits for them, and re-layouts  28 us (10%)
  starting transfers between devices  22.2 us (8%)
  between operations  14.5 us (5%)
    psum x2, waiting for transfers between devices, body(): total = lax.psum(local_sum, 'subj') / subjects  130 us
    all_to_all x1, blocking collectives, body(): lax.all_to_all(request, 'space', split_axis=1, concat_axis=1, tiled=True)  20.2 us
    all_gather x1, blocking collectives, body(): whole = lax.all_gather(template, 'subj', axis=1, tiled=True)  13.5 us
    ppermute x2, starting transfers between devices, extended(): lax.ppermute(lax.slice_in_dim(block, block.shape[dim] - width, None, axis...  8.5 us
    sub x2, other arithmetic, body(): field = field - smooth_z(rowwise)  8.33 us
    ppermute x2, starting transfers between devices, extended(): lax.ppermute(lax.slice_in_dim(block, 0, width, axis=dim), axis, backward)  7.8 us
    scatter x1, local copies, waits for them, and re-layouts, body(): request.at[jnp.arange(subj_dev)[:, None], slot].set(local_rows, mode='drop')  6.43 us
    all_to_all x1, waiting for transfers between devices, body(): lax.all_to_all(jax.vmap(lambda image, index: image[index])(images, wanted...  5.92 us
  transfers between devices with their start and end apart: 7, of which 5 were waited for; matrix products, arithmetic and copies ran while one was open for 2% of the time, Pallas kernels for 0%

commit v1 on v0

--- a/solution.py
+++ b/solution.py
@@ -121,7 +121,7 @@
         rowwise = 0.25 * padded[:, :, :-2] + 0.5 * update + 0.25 * padded[:, :, 2:]
         field = field - smooth_z(rowwise)
         local_sum = jnp.sum(predict(warped, grads, field), axis=0).reshape(rows_dev, plane, depth_z)
-        total = lax.psum(local_sum, "subj") / subjects
+        total = jnp.sum(lax.all_gather(local_sum, "subj"), axis=0) / subjects
         current = total.reshape(rows_dev, BX, BY, depth_z)
         result = lax.dynamic_slice_in_dim(total, lax.axis_index("subj") * piece, piece, 1)
     return (field.reshape(3, subj_dev, rows_dev, plane, depth_z), result)

time: 272 us -> 217 us (0.80)
  waiting for transfers between devices: 140 us -> 78.5 us
  other arithmetic: 33.1 us -> 38 us
    psum x2 -> x0, waiting for transfers between devices: 130 us -> none  [body(): total = lax.psum(local_sum, 'subj') / subjects]
    all_gather x0 -> x2, waiting for transfers between devices: none -> 68.2 us  [body(): total = jnp.sum(lax.all_gather(local_sum, 'subj'), axis=0) / subjects]
    reduce_sum x0 -> x2, other arithmetic: none -> 5.85 us  [body(): total = jnp.sum(lax.all_gather(local_sum, 'subj'), axis=0) / subjects]
where the time goes in v1:
time: 217 us; the launch traced here: 215 us
  waiting for transfers between devices  78.5 us (36%)
  other arithmetic  38 us (18%)
  blocking collectives  33.6 us (15%)
  local copies, waits for them, and re-layouts  28.1 us (13%)
  starting transfers between devices  22.2 us (10%)
  between operations  14.5 us (7%)
    all_gather x2, waiting for transfers between devices, body(): total = jnp.sum(lax.all_gather(local_sum, 'subj'), axis=0) / subjects  68.2 us
    all_to_all x1, blocking collectives, body(): lax.all_to_all(request, 'space', split_axis=1, concat_axis=1, tiled=True)  20.2 us
    all_gather x1, blocking collectives, body(): whole = lax.all_gather(template, 'subj', axis=1, tiled=True)  13.5 us
    ppermute x2, starting transfers between devices, extended(): lax.ppermute(lax.slice_in_dim(block, block.shape[dim] - width, None, axis...  8.49 us
    sub x2, other arithmetic, body(): field = field - smooth_z(rowwise)  8.33 us
    ppermute x2, starting transfers between devices, extended(): lax.ppermute(lax.slice_in_dim(block, 0, width, axis=dim), axis, backward)  7.81 us
    scatter x1, local copies, waits for them, and re-layouts, body(): request.at[jnp.arange(subj_dev)[:, None], slot].set(local_rows, mode='drop')  6.43 us
    all_to_all x1, waiting for transfers between devices, body(): lax.all_to_all(jax.vmap(lambda image, index: image[index])(images, wanted...  5.92 us
  transfers between devices with their start and end apart: 7, of which 5 were waited for; matrix products, arithmetic and copies ran while one was open for 2% of the time, Pallas kernels for 0%

profile of v1, /device:TPU:8, one launch (start us, length us, event | category | flops | bytes accessed | tf_op | source)
XLA Modules:
  0.0 214.9 jit_solution(1506527320408840879)
XLA Ops:
  7.2 0.7 subtract_bitcast_fusion
  8.0 0.8 fusion.32
  8.8 0.1 reduce_window_sum.11
  8.9 0.9 fusion.31
  9.7 0.8 fusion.38
  10.5 0.1 reshape.238
  10.6 0.8 reshape.240
  11.4 6.4 %scatter_fusion = s32[2,128]{1,0:T(2,128)S(1)} fusion(s32[2,128]{1,0:T(2,128)S(1)} %broadcast_in_dim.10, s32[128]{0:T(128)S(1)} %reshape.238, s32[128]{0:T(128)S(1)} %reshape.240), kind=kCustom, calls=%fused_computation.2 | custom fusion | bytes 2560 | tf_op jit(solution)/shard_map/scatter | solution.py:91
  17.8 0.1 reshape.222
  17.9 20.2 %all_to_all.10 = s32[2,32,4]{2,0,1:T(2,128)S(1)} all-to-all(s32[2,32,4]{2,0,1:T(2,128)S(1)} %copy.24), channel_id=1, replica_groups=mesh['subj'=8,'space'=32] {'space'}, dimensions={1} | all-to-all | bytes 2048 | tf_op jit(solution)/shard_map/all_to_all | solution.py:93
  38.1 0.1 copy.25
  38.2 0.1 copy.28
  38.3 0.1 reshape.226
  38.4 1.2 gather_fusion
  39.7 1.2 copy.29
  40.9 5.8 %all-to-all-start.1 = ((bf16[2,32,4,16,128]{4,3,2,0,1:T(8,128)(2,1)}), bf16[2,32,4,16,128]{4,3,2,0,1:T(8,128)(2,1)}, u32[]{:S(2)}, u32[]{:S(2)}) async-start(bf16[2,32,4,16,128]{4,3,2,0,1:T(8,128)(2,1)} %copy.29), calls=%async_computation.1 | async-start | bytes 2097152 | tf_op jit(solution)/shard_map/all_to_all | solution.py:94
  46.7 0.1 reshape.232
  46.8 13.5 %all_gather.9 = f32[64,16,128]{2,0,1:T(8,128)S(1)} all-gather(f32[64,2,128]{2,0,1:T(8,128)S(1)} %copy.31), channel_id=1, replica_groups=mesh['subj'=8,'space'=32] {'subj'}, dimensions={1}, use_global_device_ids=true | all-gather | bytes 589824 | tf_op jit(solution)/shard_map/all_gather | solution.py:109
  60.3 1.2 copy.32
  61.4 1.6 fusion.52
  63.0 1.1 copy-done.8
  64.1 1.7 fusion.51
  65.8 5.9 %all-to-all-done.1 = bf16[2,32,4,16,128]{4,3,2,0,1:T(8,128)(2,1)} async-done(((bf16[2,32,4,16,128]{4,3,2,0,1:T(8,128)(2,1)}), bf16[2,32,4,16,128]{4,3,2,0,1:T(8,128)(2,1)}, u32[]{:S(2)}, u32[]{:S(2)}) %all-to-all-start.1) | async-done | bytes 1048608 | tf_op jit(solution)/shard_map/all_to_all | solution.py:94
  71.8 1.4 copy.30
  73.2 0.9 gather_fusion.1
  74.1 0.1 slice.172
  74.2 0.3 slice.171
  74.5 0.3 slice.170
  74.9 0.2 pad_slice_fusion
  75.1 1.0 pad_slice_fusion.1
  76.1 0.6 pad_slice_fusion.3
  76.8 2.3 %fusion.12 = f32[2,64,4,4,128]{4,3,2,1,0:T(4,128)S(1)} fusion(f32[2,64,3,4,128]{4,3,2,1,0:T(4,128)S(1)} %slice.172, f32[2,64,4,4,128]{4,3,2,1,0:T(4,128)S(1)} %bitcast.106, f32[2,64,4,4,127]{4,3,2,1,0:T(4,128)S(1)} %get-tuple-element.35, f32[2,64,4,4,128]{4,3,2,1,0:T(4,128)S(1)} %bitcast.105, f32[2,64,4,4,128]{4,3,2,1,0:T(4,128)S(1)} %bitcast.104, ...), kind=kLoop, calls=%fused_computation.27 | loop fusion | flops 7340032 | bytes 11239936 | tf_op jit(solution)/shard_map/mul | solution.py:107
  79.1 0.6 fusion.53
  79.8 0.4 fusion.54
  80.2 0.3 fusion.55
  80.5 0.5 copy-done.14
  81.0 0.3 copy-done.15
  81.3 0.6 copy-done.16
  81.9 0.1 copy-done.19
  82.0 1.9 subtract_divide_fusion.1
  84.0 0.9 broadcast_multiply_fusion.1
  84.9 0.1 copy-done.11
  85.0 5.0 %collective-permute-start = (f32[3,2,1,4,4,128]{5,4,3,2,1,0:T(4,128)S(1)}, f32[3,2,1,4,4,128]{5,4,3,2,1,0:T(4,128)S(1)}, u32[]{:S(2)}, u32[]{:S(2)}) collective-permute-start(f32[3,2,1,4,4,128]{5,4,3,2,1,0:T(4,128)S(1)} %get-tuple-element.17), channel_id=1, source_target_pairs={{0,1},{1,2},{2,3},{3,4},{4,5},{5,6},{6,7},{7,8},{8,9},{9,10},{10,1... | collective-permute-start | bytes 147464 | tf_op jit(solution)/shard_map/ppermute | solution.py:17
  90.0 3.1 %collective-permute-start.1 = (f32[3,2,1,4,4,128]{5,4,3,2,1,0:T(4,128)S(1)}, f32[3,2,1,4,4,128]{5,4,3,2,1,0:T(4,128)S(1)}, u32[]{:S(2)}, u32[]{:S(2)}) collective-permute-start(f32[3,2,1,4,4,128]{5,4,3,2,1,0:T(4,128)S(1)} %get-tuple-element.18), channel_id=1, source_target_pairs={{1,0},{2,1},{3,2},{4,3},{5,4},{6,5},{7,6},{8,7},{9,8},{10,9},{11,1... | collective-permute-start | bytes 147464 | tf_op jit(solution)/shard_map/ppermute | solution.py:20
  93.1 2.9 %collective-permute-done.1 = f32[3,2,1,4,4,128]{5,4,3,2,1,0:T(4,128)S(1)} collective-permute-done((f32[3,2,1,4,4,128]{5,4,3,2,1,0:T(4,128)S(1)}, f32[3,2,1,4,4,128]{5,4,3,2,1,0:T(4,128)S(1)}, u32[]{:S(2)}, u32[]{:S(2)}) %collective-permute-start.1) | collective-permute-done | bytes 49184 | tf_op jit(solution)/shard_map/ppermute | solution.py:20
  96.0 2.2 %fusion.5 = f32[3,2,64,4,4,128]{5,4,3,2,1,0:T(4,128)S(1)} fusion(f32[3,2,1,4,4,128]{5,4,3,2,1,0:T(4,128)S(1)} %collective-permute-done.1, f32[3,2,64,4,4,128]{5,4,3,2,1,0:T(4,128)S(1)} %broadcast_multiply_fusion.1, f32[3,2,1,4,4,128]{5,4,3,2,1,0:T(4,128)S(1)} %collective-permute-done), kind=kLoop, calls=%fused_computation.11 | loop fusion | flops 5505024 | bytes 6389760 | tf_op jit(solution)/shard_map/add | solution.py:121
  98.3 2.1 fusion.49
  100.4 4.2 %add_subtract_fusion.1 = f32[3,2,64,4,4,128]{5,4,3,2,1,0:T(4,128)S(1)} fusion(f32[3,2,64,4,4,128]{5,4,3,2,1,0:T(4,128)S(1)} %bitcast.99, f32[3,2,64,4,4,127]{5,4,3,2,1,0:T(4,128)S(1)} %get-tuple-element.16, f32[3,2,64,4,4,127]{5,4,3,2,1,0:T(4,128)S(1)} %get-tuple-element.15, f32[3,2,1,4,4,128]{5,4,3,2,1,0:T(4,128)S(1)} %collective-permute-done.1, ...), kind=kLoop, calls=%fused_computation.17 | loop fusion | flops 10223616 | bytes 15777792 | tf_op jit(solution)/shard_map/sub | solution.py:122
  104.6 3.3 %fusion.45 = (f32[64,4,4,128]{3,2,1,0:T(4,128)}, f32[2,64,4,4,128]{4,3,2,1,0:T(4,128)}) fusion(f32[2,64,4,4,128]{4,3,2,1,0:T(4,128)S(1)} %get-tuple-element.6, f32[3,2,64,4,4,128]{5,4,3,2,1,0:T(4,128)S(1)} %add_subtract_fusion.1, f32[2,64,4,4,128]{4,3,2,1,0:T(4,128)S(1)} %fusion.12, f32[2,64,4,4,128]{4,3,2,1,0:T(4,128)S(1)} %get-tuple-element.5, ...), kind=kLoop, calls=%fused_computation.94 | loop fusion | flops 2228224 | bytes 9437184 | tf_op jit(solution)/shard_map/reduce_sum | solution.py:123
  108.0 33.5 %all-gather.3.cloned.1.call-done = f32[8,64,16,128]{3,2,1,0:T(8,128)} async-done(((f32[1,64,16,128]{3,2,1,0:T(8,128)}), f32[8,64,16,128]{3,2,1,0:T(8,128)}) %all-gather.3.cloned.1.call-update) | async-done | bytes 4194320 | tf_op jit(solution)/shard_map/all_gather | solution.py:124
  141.5 3.3 %reduce_sum.50 = f32[64,16,128]{2,1,0:T(8,128)} reduce(f32[8,64,16,128]{3,2,1,0:T(8,128)} %all-gather.3.cloned.1.call-done, f32[]{:T(128)} %constant.24.clone.1), dimensions={0}, to_apply=%region_4.5 | reduce | flops 917504 | bytes 4718596 | tf_op jit(solution)/shard_map/reduce_sum | solution.py:124
  144.8 1.1 broadcast_multiply_fusion.2
  145.9 2.6 %subtract_divide_fusion = f32[2,64,4,4,128]{4,3,2,1,0:T(4,128)S(1)} fusion(f32[2,64,4,4,128]{4,3,2,1,0:T(4,128)} %get-tuple-element.3, f32[64,4,4,128]{3,2,1,0:T(4,128)S(1)} %bitcast.111, f32[2,64,4,4,128]{4,3,2,1,0:T(4,128)} %copy-done.2, f32[2,64,4,4,128]{4,3,2,1,0:T(4,128)S(1)} %get-tuple-element.5, f32[2,64,3,4,128]{4,3,2,1,0:T(4,128)} %copy-done.6, ...), kind=kLoop, calls=%fused_computation.47 | loop fusion | flops 2621440 | bytes 6291456 | tf_op jit(solution)/shard_map/div | solution.py:116
  148.6 0.9 broadcast_multiply_fusion
  149.5 3.5 %collective-permute-start.2 = (f32[3,2,1,4,4,128]{5,4,3,2,1,0:T(4,128)S(1)}, f32[3,2,1,4,4,128]{5,4,3,2,1,0:T(4,128)S(1)}, u32[]{:S(2)}, u32[]{:S(2)}) collective-permute-start(f32[3,2,1,4,4,128]{5,4,3,2,1,0:T(4,128)S(1)} %get-tuple-element.13), channel_id=1, source_target_pairs={{0,1},{1,2},{2,3},{3,4},{4,5},{5,6},{6,7},{7,8},{8,9},{9,10},{10,1... | collective-permute-start | bytes 147464 | tf_op jit(solution)/shard_map/ppermute | solution.py:17
  153.0 4.7 %collective-permute-start.3 = (f32[3,2,1,4,4,128]{5,4,3,2,1,0:T(4,128)S(1)}, f32[3,2,1,4,4,128]{5,4,3,2,1,0:T(4,128)S(1)}, u32[]{:S(2)}, u32[]{:S(2)}) collective-permute-start(f32[3,2,1,4,4,128]{5,4,3,2,1,0:T(4,128)S(1)} %get-tuple-element.14), channel_id=1, source_target_pairs={{1,0},{2,1},{3,2},{4,3},{5,4},{6,5},{7,6},{8,7},{9,8},{10,9},{11,1... | collective-permute-start | bytes 147464 | tf_op jit(solution)/shard_map/ppermute | solution.py:20
  157.7 1.5 collective-permute-done.3
  159.2 2.2 %fusion.1 = f32[3,2,64,4,4,128]{5,4,3,2,1,0:T(4,128)S(1)} fusion(f32[3,2,1,4,4,128]{5,4,3,2,1,0:T(4,128)S(1)} %collective-permute-done.3, f32[3,2,64,4,4,128]{5,4,3,2,1,0:T(4,128)S(1)} %broadcast_multiply_fusion, f32[3,2,1,4,4,128]{5,4,3,2,1,0:T(4,128)S(1)} %collective-permute-done.2), kind=kLoop, calls=%fused_computation.5 | loop fusion | flops 5505024 | bytes 6389760 | tf_op jit(solution)/shard_map/add | solution.py:121
  161.4 2.1 fusion.47
  163.6 4.2 %add_subtract_fusion = f32[3,2,64,4,4,128]{5,4,3,2,1,0:T(4,128)S(1)} fusion(f32[3,2,64,4,4,128]{5,4,3,2,1,0:T(4,128)S(1)} %copy-done.5, f32[3,2,64,4,4,127]{5,4,3,2,1,0:T(4,128)S(1)} %get-tuple-element.12, f32[3,2,64,4,4,127]{5,4,3,2,1,0:T(4,128)S(1)} %get-tuple-element.11, f32[3,2,1,4,4,128]{5,4,3,2,1,0:T(4,128)S(1)} %collective-permute-done.3, ...), kind=kLoop, calls=%fused_computation.16 | loop fusion | flops 10223616 | bytes 15777792 | tf_op jit(solution)/shard_map/sub | solution.py:122
  167.8 2.3 %fusion.15 = f32[64,4,4,128]{3,2,1,0:T(4,128)} fusion(f32[2,64,4,4,128]{4,3,2,1,0:T(4,128)S(1)} %copy-done.3, f32[3,2,64,4,4,128]{5,4,3,2,1,0:T(4,128)S(1)} %add_subtract_fusion, f32[2,64,4,4,128]{4,3,2,1,0:T(4,128)S(1)} %fusion.12, f32[2,64,4,4,128]{4,3,2,1,0:T(4,128)S(1)} %get-tuple-element.5, f32[2,64,3,4,128]{4,3,2,1,0:T(4,128)S(1)} %copy-done.7, ...), kind=kLoop, calls=%fused_computation.31 | loop fusion | flops 2228224 | bytes 8388608 | tf_op jit(solution)/shard_map/reduce_sum | solution.py:123
  170.2 34.7 %all-gather.5.cloned.1.call-done = f32[8,64,16,128]{3,2,1,0:T(8,128)} async-done(((f32[1,64,16,128]{3,2,1,0:T(8,128)}), f32[8,64,16,128]{3,2,1,0:T(8,128)}) %all-gather.5.cloned.1.call-update) | async-done | bytes 4194320 | tf_op jit(solution)/shard_map/all_gather | solution.py:124
  204.9 2.5 %reduce_sum.52 = f32[64,16,128]{2,1,0:T(8,128)S(1)} reduce(f32[8,64,16,128]{3,2,1,0:T(8,128)} %all-gather.5.cloned.1.call-done, f32[]{:T(128)} %constant.24.clone.1), dimensions={0}, to_apply=%region_6.7 | reduce | flops 917504 | bytes 4718596 | tf_op jit(solution)/shard_map/reduce_sum | solution.py:124
  207.4 0.7 dynamic-slice_multiply_fusion
  (50 shorter events, 0.4 us)
Async XLA Ops:
  7.2 31.3 %copy-start = (bf16[2,64,16,128]{3,2,1,0:T(8,128)(2,1)S(1)}, bf16[2,64,16,128]{3,2,1,0:T(8,128)(2,1)}, u32[]{:S(2)}) copy-start(bf16[2,64,16,128]{3,2,1,0:T(8,128)(2,1)} %param.7) | copy-start | bytes 1572868
  38.4 8.4 %copy-start.20 = (f32[64,2,128]{2,1,0:T(2,128)S(1)}, f32[64,2,128]{2,1,0:T(2,128)}, u32[]{:S(2)}) copy-start(f32[64,2,128]{2,1,0:T(2,128)} %param.10) | copy-start | bytes 196612
  39.7 21.8 %copy-start.13 = (bf16[3,2,64,16,128]{4,3,2,1,0:T(8,128)(2,1)S(1)}, bf16[3,2,64,16,128]{4,3,2,1,0:T(8,128)(2,1)}, u32[]{:S(2)}) copy-start(bf16[3,2,64,16,128]{4,3,2,1,0:T(8,128)(2,1)} %param.9) | copy-start | bytes 4718596
  40.9 30.8 %all-to-all-start.1 = ((bf16[2,32,4,16,128]{4,3,2,0,1:T(8,128)(2,1)}), bf16[2,32,4,16,128]{4,3,2,0,1:T(8,128)(2,1)}, u32[]{:S(2)}, u32[]{:S(2)}) async-start(bf16[2,32,4,16,128]{4,3,2,0,1:T(8,128)(2,1)} %copy.29), calls=%async_computation.1 | async-start | bytes 2097152 | tf_op jit(solution)/shard_map/all_to_all | solution.py:94
  46.7 94.8 %all-gather.3.cloned.1.call-start = ((), (), s32[]{:S(2)}) async-start(), calls=%async_computation.2 | async-start | bytes 4718592 | tf_op jit(solution)/shard_map/all_gather | solution.py:124
  61.4 2.6 %copy-start.8 = (f32[3,2,64,16,128]{4,3,2,1,0:T(8,128)S(1)}, f32[3,2,64,16,128]{4,3,2,1,0:T(8,128)}, u32[]{:S(2)}) copy-start(f32[3,2,64,16,128]{4,3,2,1,0:T(8,128)} %param.8) | copy-start | bytes 9437188
  75.1 1.6 copy-start.17
  75.1 1.6 copy-start.18
  79.7 1.2 copy-start.14
  79.7 1.5 copy-start.15
  79.8 2.1 copy-start.16
  79.8 2.2 %copy-start.19 = (f32[64,4,4,128]{3,2,1,0:T(4,128)S(1)}, f32[64,4,4,128]{3,2,1,0:T(4,128)}, u32[]{:S(2)}) copy-start(f32[64,4,4,128]{3,2,1,0:T(4,128)} %copy.32) | copy-start | bytes 1572868
  80.5 24.1 %copy-start.6 = (f32[2,64,3,4,128]{4,3,2,1,0:T(4,128)}, f32[2,64,3,4,128]{4,3,2,1,0:T(4,128)S(1)}, u32[]{:S(2)}) copy-start(f32[2,64,3,4,128]{4,3,2,1,0:T(4,128)S(1)} %get-tuple-element.31) | copy-start | bytes 2359300
  84.0 1.0 copy-start.11
  84.0 20.6 %copy-start.2 = (f32[2,64,4,4,128]{4,3,2,1,0:T(4,128)}, f32[2,64,4,4,128]{4,3,2,1,0:T(4,128)S(1)}, u32[]{:S(2)}) copy-start(f32[2,64,4,4,128]{4,3,2,1,0:T(4,128)S(1)} %get-tuple-element.6) | copy-start | bytes 3145732
  85.0 8.1 %collective-permute-start = (f32[3,2,1,4,4,128]{5,4,3,2,1,0:T(4,128)S(1)}, f32[3,2,1,4,4,128]{5,4,3,2,1,0:T(4,128)S(1)}, u32[]{:S(2)}, u32[]{:S(2)}) collective-permute-start(f32[3,2,1,4,4,128]{5,4,3,2,1,0:T(4,128)S(1)} %get-tuple-element.17), channel_id=1, source_target_pairs={{0,1},{1,2},{2,3},{3,4},{4,5},{5,6},{6,7},{7,8},{8,9},{9,10},{10,1... | collective-permute-start | bytes 147464 | tf_op jit(solution)/shard_map/ppermute | solution.py:17
  90.0 6.0 %collective-permute-start.1 = (f32[3,2,1,4,4,128]{5,4,3,2,1,0:T(4,128)S(1)}, f32[3,2,1,4,4,128]{5,4,3,2,1,0:T(4,128)S(1)}, u32[]{:S(2)}, u32[]{:S(2)}) collective-permute-start(f32[3,2,1,4,4,128]{5,4,3,2,1,0:T(4,128)S(1)} %get-tuple-element.18), channel_id=1, source_target_pairs={{1,0},{2,1},{3,2},{4,3},{5,4},{6,5},{7,6},{8,7},{9,8},{10,9},{11,1... | collective-permute-start | bytes 147464 | tf_op jit(solution)/shard_map/ppermute | solution.py:20
  98.3 2.2 %copy-start.9 = (f32[3,2,64,16,128]{4,3,2,1,0:T(8,128)S(1)}, f32[3,2,64,16,128]{4,3,2,1,0:T(8,128)}, u32[]{:S(2)}) copy-start(f32[3,2,64,16,128]{4,3,2,1,0:T(8,128)} %param.8) | copy-start | bytes 9437188
  104.6 3.3 %copy-start.4 = (f32[3,2,64,4,4,128]{5,4,3,2,1,0:T(4,128)}, f32[3,2,64,4,4,128]{5,4,3,2,1,0:T(4,128)S(1)}, u32[]{:S(2)}) copy-start(f32[3,2,64,4,4,128]{5,4,3,2,1,0:T(4,128)S(1)} %add_subtract_fusion.1) | copy-start | bytes 9437188
  108.0 96.9 %all-gather.5.cloned.1.call-start = ((), (), s32[]{:S(2)}) async-start(), calls=%async_computation.3 | async-start | bytes 4718592 | tf_op jit(solution)/shard_map/all_gather | solution.py:124
  145.9 2.7 %copy-start.3 = (f32[2,64,4,4,128]{4,3,2,1,0:T(4,128)S(1)}, f32[2,64,4,4,128]{4,3,2,1,0:T(4,128)}, u32[]{:S(2)}) copy-start(f32[2,64,4,4,128]{4,3,2,1,0:T(4,128)} %copy-done.2) | copy-start | bytes 3145732
  145.9 2.7 %copy-start.12 = (f32[1,2,64,4,4,128]{5,4,3,2,1,0:T(4,128)S(1)}, f32[1,2,64,4,4,128]{5,4,3,2,1,0:T(4,128)}, u32[]{:S(2)}) copy-start(f32[1,2,64,4,4,128]{5,4,3,2,1,0:T(4,128)} %copy-done.11) | copy-start | bytes 3145732
  149.5 8.2 %collective-permute-start.2 = (f32[3,2,1,4,4,128]{5,4,3,2,1,0:T(4,128)S(1)}, f32[3,2,1,4,4,128]{5,4,3,2,1,0:T(4,128)S(1)}, u32[]{:S(2)}, u32[]{:S(2)}) collective-permute-start(f32[3,2,1,4,4,128]{5,4,3,2,1,0:T(4,128)S(1)} %get-tuple-element.13), channel_id=1, source_target_pairs={{0,1},{1,2},{2,3},{3,4},{4,5},{5,6},{6,7},{7,8},{8,9},{9,10},{10,1... | collective-permute-start | bytes 147464 | tf_op jit(solution)/shard_map/ppermute | solution.py:17
  153.0 6.2 %collective-permute-start.3 = (f32[3,2,1,4,4,128]{5,4,3,2,1,0:T(4,128)S(1)}, f32[3,2,1,4,4,128]{5,4,3,2,1,0:T(4,128)S(1)}, u32[]{:S(2)}, u32[]{:S(2)}) collective-permute-start(f32[3,2,1,4,4,128]{5,4,3,2,1,0:T(4,128)S(1)} %get-tuple-element.14), channel_id=1, source_target_pairs={{1,0},{2,1},{3,2},{4,3},{5,4},{6,5},{7,6},{8,7},{9,8},{10,9},{11,1... | collective-permute-start | bytes 147464 | tf_op jit(solution)/shard_map/ppermute | solution.py:20
  161.4 2.2 %copy-start.5 = (f32[3,2,64,4,4,128]{5,4,3,2,1,0:T(4,128)S(1)}, f32[3,2,64,4,4,128]{5,4,3,2,1,0:T(4,128)}, u32[]{:S(2)}) copy-start(f32[3,2,64,4,4,128]{5,4,3,2,1,0:T(4,128)} %copy-done.4) | copy-start | bytes 9437188
  163.6 4.2 %copy-start.7 = (f32[2,64,3,4,128]{4,3,2,1,0:T(4,128)S(1)}, f32[2,64,3,4,128]{4,3,2,1,0:T(4,128)}, u32[]{:S(2)}) copy-start(f32[2,64,3,4,128]{4,3,2,1,0:T(4,128)} %copy-done.6) | copy-start | bytes 2359300
  167.8 2.3 %copy-start.10 = (f32[3,2,64,4,4,128]{5,4,3,2,1,0:T(4,128)}, f32[3,2,64,4,4,128]{5,4,3,2,1,0:T(4,128)S(1)}, u32[]{:S(2)}) copy-start(f32[3,2,64,4,4,128]{5,4,3,2,1,0:T(4,128)S(1)} %add_subtract_fusion) | copy-start | bytes 9437188
  167.8 40.2 %copy-start.1 = (bf16[2,64,16,128]{3,2,1,0:T(8,128)(2,1)S(1)}, bf16[2,64,16,128]{3,2,1,0:T(8,128)(2,1)}, u32[]{:S(2)}) copy-start(bf16[2,64,16,128]{3,2,1,0:T(8,128)(2,1)} %param.7) | copy-start | bytes 1572868
Sparse Core Ops, SparseCore 0:
  108.1 33.3 all-gather.2
  170.3 34.5 all-gather.4
